TPU v7x, 32 devices: a whole 2x2x4 slice. The times are simulated.
32 devices in a mesh: db: 8 (over y, x, core), pb: 4 (over z).
Axes of the slice: x: 2, y: 2, z: 4, core: 2. Of those that a mesh axis runs over, the one named last changes fastest.
Arguments:
- query_maps: bfloat16 [32, 256, 256], P(('db', 'pb')), may hold values from -6 to 6
- database: bfloat16 [1024, 256, 256], P(('db', 'pb')), may hold values from -6 to 6
- shortlist: int32 [32, 128], P(('db', 'pb')), may hold values from 0 to 1023, as said below
- kernel_query: bfloat16 [3, 3], replicated, may hold values from -1.5 to 1.5
- kernel_db: bfloat16 [3, 3], replicated, may hold values from -1.5 to 1.5
Outputs:
- scores: float32 [32, 128], P(('db', 'pb'))
- top_scores: float32 [32, 100], P(('db', 'pb'))
Inputs may be any that keep to these rules, and one draw needn't show every extreme that they name: Within one query the ids are distinct. Among the 128 shortlist entries of the query held by device q (query q), at most 8 lie in any one shard of images (ids s * 32 to (s + 1) * 32 - 1), and some shard holds exactly 8 of them for every device.
All inputs are finite; a program needn't handle non-finite values.
Results may differ from a plain program's by a relative error of at most 0.0003.
Values may be sent and summed in bfloat16 or wider, within the bound.
A program may use at most 128 MiB of HBM per device.

v0:
```python
import functools

import jax
import jax.numpy as jnp
from jax import lax
from jax.experimental import pallas as pl
from jax.experimental.pallas import tpu as pltpu
from jax.sharding import PartitionSpec as P

GRID = 16
TOPK = 100
LANES = 128
ROWS = 8
MESH = pl.DeviceIdType.MESH

epsilon = 1e-06
score_scale = 8.0


def unit_map(values):
    squares = jnp.sum(values * values, axis=0, keepdims=True)
    return values * lax.rsqrt(squares + epsilon)


def fill_filters(query_taps, db_taps, filter_query, filter_db):
    cells = filter_query.shape[0]
    row = lax.broadcasted_iota(jnp.int32, (cells, cells), 0)
    col = lax.broadcasted_iota(jnp.int32, (cells, cells), 1)
    down = (col >> 4) - (row >> 4)
    across = (col & (GRID - 1)) - (row & (GRID - 1))
    near = (jnp.abs(down) <= 1) & (jnp.abs(across) <= 1)
    tap = jnp.where(near, down * 3 + across + 4, -1)
    query_matrix = jnp.zeros((cells, cells), jnp.float32)
    db_matrix = jnp.zeros((cells, cells), jnp.float32)
    query_values = query_taps[...].astype(jnp.float32)
    db_values = db_taps[...].astype(jnp.float32)
    for i in range(3):
        for j in range(3):
            hit = tap == 3 * i + j
            back = tap == 8 - (3 * i + j)
            query_matrix = jnp.where(hit, query_values[i : i + 1, j : j + 1], query_matrix)
            db_matrix = jnp.where(back, db_values[i : i + 1, j : j + 1], db_matrix)
    filter_query[...] = query_matrix.astype(jnp.bfloat16)
    filter_db[...] = db_matrix.astype(jnp.bfloat16)


def shortlist_info(ids, image_count, count):
    entries = ids.shape[1]
    shard = jnp.zeros_like(ids)
    for s in range(1, count):
        shard = shard + jnp.where(ids >= s * image_count, 1, 0)
    slot = ids - shard * image_count
    across = jnp.broadcast_to(shard, (entries, entries))
    above = lax.broadcasted_iota(jnp.int32, (entries, entries), 0)
    beside = lax.broadcasted_iota(jnp.int32, (entries, entries), 1)
    earlier = (across.T == across) & (above < beside)
    bucket = jnp.sum(jnp.where(earlier, 1, 0), axis=0, keepdims=True)
    rank = lax.broadcasted_iota(jnp.int32, (ROWS, entries), 0)
    return jnp.where(rank == 0, shard, jnp.where(rank == 1, slot, bucket))


def descending(row):
    entries = row.shape[1]
    across = jnp.broadcast_to(row, (entries, entries))
    down = across.T
    above = lax.broadcasted_iota(jnp.int32, (entries, entries), 0)
    beside = lax.broadcasted_iota(jnp.int32, (entries, entries), 1)
    ahead = (down > across) | ((down == across) & (above < beside))
    rank = jnp.sum(jnp.where(ahead, 1.0, 0.0), axis=0, keepdims=True)
    rank_down = jnp.broadcast_to(rank, (entries, entries)).T
    chosen = jnp.where(rank_down == beside.astype(jnp.float32), down, 0.0)
    return jnp.sum(chosen, axis=0, keepdims=True)


def kernel(
    db_count,
    pb_count,
    width,
    query_ref,
    shortlist_ref,
    database_ref,
    query_taps,
    db_taps,
    out_ref,
    sorted_ref,
    filter_query,
    filter_db,
    raw,
    positive,
    maps,
    infos,
    units,
    slot_rows,
    slot_table,
    own_rows,
    own_table,
    current,
    peaks,
    found,
    returned,
    map_send,
    map_recv,
    info_send,
    info_recv,
    back_send,
    back_recv,
    local_sem,
    own_sem,
    raw_sem,
):
    count = db_count * pb_count
    chips = db_count // 2
    image_count = database_ref.shape[0]
    db = lax.axis_index("db")
    pb = lax.axis_index("pb")
    chip = db // 2
    core = lax.rem(db, 2)
    me = db * pb_count + pb

    def place(index):
        return (index // pb_count, lax.rem(index, pb_count))

    def index_of(other_pb, other_chip, other_core):
        return (other_chip * 2 + other_core) * pb_count + other_pb

    def map_copy(source, block, send_slot, device):
        return pltpu.make_async_remote_copy(
            src_ref=block,
            dst_ref=maps.at[source],
            send_sem=map_send.at[send_slot],
            recv_sem=map_recv.at[source],
            device_id=device,
            device_id_type=MESH,
        )

    def info_copy(other, owner):
        return pltpu.make_async_remote_copy(
            src_ref=infos.at[me],
            dst_ref=infos.at[owner],
            send_sem=info_send.at[other],
            recv_sem=info_recv.at[owner],
            device_id=place(other),
            device_id_type=MESH,
        )

    def back_copy(source, landed):
        return pltpu.make_async_remote_copy(
            src_ref=found.at[source],
            dst_ref=returned.at[landed],
            send_sem=back_send.at[source],
            recv_sem=back_recv.at[landed],
            device_id=place(source),
            device_id_type=MESH,
        )

    def raw_copy(image):
        return pltpu.make_async_copy(database_ref.at[image], raw.at[image], raw_sem.at[image])

    barrier = pltpu.get_barrier_semaphore()

    @pl.loop(1, count)
    def _(step):
        pl.semaphore_signal(
            barrier, inc=1, device_id=place(lax.rem(me + step, count)), device_id_type=MESH
        )

    @pl.loop(0, image_count)
    def _(image):
        raw_copy(image).start()

    maps[me] = unit_map(query_ref[0].astype(jnp.float32)).T.astype(jnp.bfloat16)
    my_info = shortlist_info(shortlist_ref[...], image_count, count)
    infos[me] = my_info
    rank = lax.broadcasted_iota(jnp.int32, (ROWS, LANES), 0)
    spot = lax.broadcasted_iota(jnp.int32, (ROWS, LANES), 1)
    own = jnp.zeros((ROWS, LANES), jnp.int32)
    for k in range(width):
        hit = (my_info[0:1, :] == me) & (my_info[2:3, :] == k)
        slot = jnp.sum(jnp.where(hit, my_info[1:2, :], 0), axis=1, keepdims=True)
        own = jnp.where(spot == k, slot, own)
    own_rows[...] = own
    own_smem = pltpu.make_async_copy(own_rows, own_table, own_sem)
    own_smem.start()
    fill_filters(query_taps, db_taps, filter_query, filter_db)
    peaks[...] = jnp.zeros_like(peaks)
    first_half = image_count // 2

    def normalize(image):
        raw_copy(image).wait()
        units[image] = unit_map(raw[image].astype(jnp.float32)).astype(jnp.bfloat16)

    pl.loop(0, first_half)(normalize)
    pl.semaphore_wait(barrier, count - 1)

    plane_base = pb_count
    partner_base = pb_count + pb_count * chips

    @pl.loop(1, count)
    def _(step):
        info_copy(lax.rem(me + step, count), me).start()

    for step in range(1, pb_count):
        map_copy(me, maps.at[me], step, (db, lax.rem(pb + step, pb_count))).start()
    for step in range(1, chips):
        map_copy(
            me, maps.at[me], plane_base + step, (lax.rem(chip + step, chips) * 2 + core, pb)
        ).start()

    map_copy(me, maps.at[me], partner_base, (chip * 2 + 1 - core, pb)).start()

    pl.loop(first_half, image_count)(normalize)
    own_smem.wait()

    def fill_slots():
        @pl.loop(1, count)
        def _(step):
            info_copy(lax.rem(me + step, count), lax.rem(me + step, count)).wait_recv()

        shard_of = infos[:, 0, :]
        slot_of = infos[:, 1, :]
        bucket_of = infos[:, 2, :]
        lane = lax.broadcasted_iota(jnp.int32, (count, LANES), 1)
        table = jnp.zeros((count, LANES), jnp.int32)
        for k in range(width):
            hit = (shard_of == me) & (bucket_of == k)
            slot = jnp.sum(jnp.where(hit, slot_of, 0), axis=1, keepdims=True)
            table = jnp.where(lane == k, slot, table)
        slot_rows[...] = table
        to_smem = pltpu.make_async_copy(slot_rows, slot_table, local_sem)
        to_smem.start()
        to_smem.wait()

    @pl.loop(0, count)
    def _(turn):
        place_in = turn + (turn + count - 1) // count - (count - 1) * ((turn + 1) // count)
        step = place_in // 2
        half = lax.rem(place_in, 2)
        hop = lax.rem(step, chips)
        other_pb = lax.rem(pb + step // chips, pb_count)
        other_chip = lax.rem(chip + hop, chips)
        source = index_of(other_pb, other_chip, lax.rem(core + half, 2))

        @pl.when((half == 0) & (step >= 1) & (step < pb_count))
        def _():
            line_pb = lax.rem(pb + step, pb_count)
            line = index_of(line_pb, chip, core)
            map_copy(line, maps.at[line], 0, (db, line_pb)).wait_recv()
            for d in range(1, chips):
                map_copy(
                    line,
                    maps.at[line],
                    plane_base + step * chips + d,
                    (lax.rem(chip + d, chips) * 2 + core, pb),
                ).start()

        @pl.when((half == 1) | (hop != 0))
        def _():
            map_copy(source, maps.at[source], 0, (chip * 2 + 1 - core, pb)).wait_recv()

        @pl.when((half == 0) & (step != 0))
        def _():
            map_copy(
                source, maps.at[source], partner_base + step, (chip * 2 + 1 - core, pb)
            ).start()

        @pl.when(turn == 0)
        def _():
            for k in range(width):
                current[k] = own_table[0, k]

        @pl.when(turn == 1)
        def _():
            fill_slots()

        @pl.when(turn != 0)
        def _():
            for k in range(width):
                current[k] = slot_table[source, k]

        for k in range(width):
            slot = current[k]
            correlation = jnp.dot(
                maps[source], units[slot], preferred_element_type=jnp.float32
            )
            positive[k] = jnp.maximum(correlation, 0.0).astype(jnp.bfloat16)
        for k in range(width):
            rectified = positive[k]
            filtered = jnp.dot(
                filter_query[...], rectified, preferred_element_type=jnp.float32
            ) + jnp.dot(rectified, filter_db[...], preferred_element_type=jnp.float32)
            peaks[k : k + 1, :] = jnp.max(filtered, axis=0, keepdims=True)
        best = peaks[...]
        total = jnp.sum(best, axis=1, keepdims=True) * (score_scale / best.shape[1])
        found[source] = jnp.broadcast_to(total, (ROWS, LANES))

        @pl.when(source != me)
        def _():
            back_copy(source, me).start()

    returned[me] = found[me]

    @pl.loop(1, count)
    def _(step):
        other = lax.rem(me + step, count)
        back_copy(other, other).wait_recv()

    my_shard = my_info[0:1, :]
    my_bucket = my_info[2:3, :]
    scores = jnp.zeros((ROWS, LANES), jnp.float32)
    for s in range(count):
        scores = scores + jnp.where((my_shard == s) & (my_bucket == rank), returned[s], 0.0)
    final = jnp.sum(scores, axis=0, keepdims=True)
    out_ref[...] = final
    sorted_ref[...] = descending(final)

    @pl.loop(1, count)
    def _(step):
        other = lax.rem(me + step, count)
        info_copy(other, me).wait_send()
        back_copy(other, me).wait_send()

    for step in range(1, pb_count):
        map_copy(me, maps.at[me], step, (db, pb)).wait_send()
    for step in range(pb_count):
        for d in range(1, chips):
            map_copy(me, maps.at[me], plane_base + step * chips + d, (db, pb)).wait_send()

    @pl.loop(0, pb_count * chips)
    def _(step):
        map_copy(me, maps.at[me], partner_base + step, (db, pb)).wait_send()


def body(db_count, pb_count, query_maps, database, shortlist, kernel_query, kernel_db):
    count = db_count * pb_count
    chips = db_count // 2
    image_count, channels, cells = database.shape
    entries = shortlist.shape[1]
    width = 2 * entries // count
    vmem = pl.BlockSpec(memory_space=pltpu.VMEM)
    row = jax.ShapeDtypeStruct((1, entries), jnp.float32)
    scores, ordered = pl.pallas_call(
        functools.partial(kernel, db_count, pb_count, width),
        out_shape=(row, row),
        in_specs=[vmem, vmem, pl.BlockSpec(memory_space=pl.ANY), vmem, vmem],
        out_specs=(vmem, vmem),
        scratch_shapes=[
            pltpu.VMEM((cells, cells), jnp.bfloat16),
            pltpu.VMEM((cells, cells), jnp.bfloat16),
            pltpu.VMEM((image_count, channels, cells), jnp.bfloat16),
            pltpu.VMEM((width, cells, cells), jnp.bfloat16),
            pltpu.VMEM((count, cells, channels), jnp.bfloat16),
            pltpu.VMEM((count, ROWS, LANES), jnp.int32),
            pltpu.VMEM((image_count, channels, cells), jnp.bfloat16),
            pltpu.VMEM((count, LANES), jnp.int32),
            pltpu.SMEM((count, LANES), jnp.int32),
            pltpu.VMEM((ROWS, LANES), jnp.int32),
            pltpu.SMEM((ROWS, LANES), jnp.int32),
            pltpu.SMEM((width,), jnp.int32),
            pltpu.VMEM((ROWS, cells), jnp.float32),
            pltpu.VMEM((count, ROWS, LANES), jnp.float32),
            pltpu.VMEM((count, ROWS, LANES), jnp.float32),
            pltpu.SemaphoreType.DMA((pb_count + 2 * pb_count * chips,)),
            pltpu.SemaphoreType.DMA((count,)),
            pltpu.SemaphoreType.DMA((count,)),
            pltpu.SemaphoreType.DMA((count,)),
            pltpu.SemaphoreType.DMA((count,)),
            pltpu.SemaphoreType.DMA((count,)),
            pltpu.SemaphoreType.DMA,
            pltpu.SemaphoreType.DMA,
            pltpu.SemaphoreType.DMA((image_count,)),
        ],
        compiler_params=pltpu.CompilerParams(
            collective_id=0, has_side_effects=True, vmem_limit_bytes=56 * 1024 * 1024
        ),
    )(query_maps, shortlist, database, kernel_query, kernel_db)
    return (scores, ordered[:, :TOPK])


def solution(mesh):
    in_specs = (
        P(("db", "pb"), None, None),
        P(("db", "pb"), None, None),
        P(("db", "pb"), None),
        P(),
        P(),
    )
    out_specs = (P(("db", "pb"), None), P(("db", "pb"), None))
    step = functools.partial(body, mesh.shape["db"], mesh.shape["pb"])
    return jax.shard_map(step, mesh=mesh, in_specs=in_specs, out_specs=out_specs, check_vma=False)
```

profile of v0, /device:TPU:0, one launch (start us, length us, event | category | flops | bytes accessed | tf_op | source)
XLA Modules:
  0.0 65.9 jit_solution(2864461006778642647)
XLA Ops:
  0.6 63.0 %shard_map.68 = (f32[1,128]{1,0:T(1,128)}, f32[1,128]{1,0:T(1,128)}) custom-call(bf16[1,256,256]{2,1,0:T(8,128)(2,1)} %query_ref.1, s32[1,128]{1,0:T(1,128)} %shortlist_ref.1, bf16[32,256,256]{2,1,0:T(8,128)(2,1)} %database_ref.1, bf16[3,3]{1,0:T(4,128)(2,1)} %query_taps.1, bf16[3,3]{1,0:T(4,128)(2,1)} %db_taps.1), custom_call_target="tpu_custom_call" | custom-call | tf_op jit(solution)/shard_map/pallas_call | solution.py:341
  63.7 1.1 %copy.9 = f32[1,128]{1,0:T(1,128)} copy(f32[1,128]{1,0:T(1,128)} %get-tuple-element.8) | data formatting | bytes 1024
  64.8 1.1 %copy.10 = f32[1,100]{1,0:T(1,128)} copy(f32[1,100]{1,0:T(1,128)} %bitcast.1) | data formatting | bytes 800
where the time goes:
time: 66.1 us; the launch traced here: 65.9 us
  Pallas kernels  63 us (95%)
  local copies, waits for them, and re-layouts  2.25 us (3%)
    pallas_call x1, Pallas kernels, body(): pl.pallas_call(functools.partial(kernel, db_count, pb_count, width), out_...  63 us
    unnamed x2, local copies, waits for them, and re-layouts  2.25 us

commit v1 on v0

v1 whole, which is shorter than its diff:
```python
import functools
import math

import jax
import jax.numpy as jnp
from jax import lax
from jax.experimental import pallas as pl
from jax.experimental.pallas import tpu as pltpu
from jax.sharding import PartitionSpec as P

GRID = 16
TOPK = 100
LANES = 128
ROWS = 8
TAIL = 16
EARLY = 2
MESH = pl.DeviceIdType.MESH

epsilon = 1e-06
score_scale = 8.0


def unit_map(values):
    squares = jnp.sum(values * values, axis=0, keepdims=True)
    return values * lax.rsqrt(squares + epsilon)


def fill_filters(query_taps, db_taps, filter_query, filter_db):
    cells = filter_query.shape[0]
    row = lax.broadcasted_iota(jnp.int32, (cells, cells), 0)
    col = lax.broadcasted_iota(jnp.int32, (cells, cells), 1)
    down = (col >> 4) - (row >> 4)
    across = (col & (GRID - 1)) - (row & (GRID - 1))
    near = (jnp.abs(down) <= 1) & (jnp.abs(across) <= 1)
    tap = jnp.where(near, down * 3 + across + 4, -1)
    query_matrix = jnp.zeros((cells, cells), jnp.float32)
    db_matrix = jnp.zeros((cells, cells), jnp.float32)
    query_values = query_taps[...].astype(jnp.float32)
    db_values = db_taps[...].astype(jnp.float32)
    for i in range(3):
        for j in range(3):
            hit = tap == 3 * i + j
            back = tap == 8 - (3 * i + j)
            query_matrix = jnp.where(hit, query_values[i : i + 1, j : j + 1], query_matrix)
            db_matrix = jnp.where(back, db_values[i : i + 1, j : j + 1], db_matrix)
    filter_query[...] = query_matrix.astype(jnp.bfloat16)
    filter_db[...] = db_matrix.astype(jnp.bfloat16)


def shortlist_info(ids, image_count, count):
    entries = ids.shape[1]
    shard = jnp.zeros_like(ids)
    for s in range(1, count):
        shard = shard + jnp.where(ids >= s * image_count, 1, 0)
    slot = ids - shard * image_count
    across = jnp.broadcast_to(shard, (entries, entries))
    above = lax.broadcasted_iota(jnp.int32, (entries, entries), 0)
    beside = lax.broadcasted_iota(jnp.int32, (entries, entries), 1)
    earlier = (across.T == across) & (above < beside)
    bucket = jnp.sum(jnp.where(earlier, 1, 0), axis=0, keepdims=True)
    rank = lax.broadcasted_iota(jnp.int32, (TAIL, entries), 0)
    return jnp.where(rank == 0, shard, jnp.where(rank == 1, slot, bucket))


def descending(row):
    entries = row.shape[1]
    across = jnp.broadcast_to(row, (entries, entries))
    down = across.T
    above = lax.broadcasted_iota(jnp.int32, (entries, entries), 0)
    beside = lax.broadcasted_iota(jnp.int32, (entries, entries), 1)
    ahead = (down > across) | ((down == across) & (above < beside))
    rank = jnp.sum(jnp.where(ahead, 1.0, 0.0), axis=0, keepdims=True)
    rank_down = jnp.broadcast_to(rank, (entries, entries)).T
    chosen = jnp.where(rank_down == beside.astype(jnp.float32), down, 0.0)
    return jnp.sum(chosen, axis=0, keepdims=True)


def flip(a, b, size):
    total = 0
    bit = 1
    while bit < size:
        total = total + lax.rem(a // bit + b // bit, 2) * bit
        bit *= 2
    return total


def combo_order(side, line):
    order = []
    for wave in range(line + 2):
        for v in range(side):
            for u in range(side):
                j = wave - min(u, 1) - min(v, 1)
                if 0 <= j < line:
                    order.append((j * side + u) * side + v)
    return order


def kernel(
    db_count,
    pb_count,
    width,
    query_any,
    shortlist_ref,
    database_ref,
    query_taps,
    db_taps,
    out_ref,
    sorted_ref,
    filter_query,
    filter_db,
    raw,
    positive,
    maps,
    info,
    units,
    slot_rows,
    slot_table,
    peaks,
    found,
    returned,
    query_ref,
    map_send,
    map_recv,
    back_send,
    back_recv,
    slot_sem,
    raw_sem,
    query_sem,
):
    count = db_count * pb_count
    chips = db_count // 2
    side = math.isqrt(chips)
    combos = pb_count * chips
    order = combo_order(side, pb_count)
    image_count = database_ref.shape[0]
    cells = units.shape[2]
    db = lax.axis_index("db")
    pb = lax.axis_index("pb")
    chip = db // 2
    core = lax.rem(db, 2)
    me = db * pb_count + pb
    partner = (chip * 2 + 1 - core, pb)
    first_stride = 1 + core * (side - 1)
    second_stride = side - core * (side - 1)

    first_base = pb_count - 1
    second_base = first_base + pb_count * (side - 1)
    partner_base = second_base + pb_count * side * (side - 1)
    sends = partner_base + combos

    def place(index):
        return (index // pb_count, lax.rem(index, pb_count))

    def line_peer(j):
        return (db, flip(pb, j, pb_count))

    def first_peer(u):
        return (flip(chip, u * first_stride, chips) * 2 + core, pb)

    def second_peer(v):
        return (flip(chip, v * second_stride, chips) * 2 + core, pb)

    def map_copy(source, send_slot, device):
        return pltpu.make_async_remote_copy(
            src_ref=maps.at[source],
            dst_ref=maps.at[source],
            send_sem=map_send.at[send_slot],
            recv_sem=map_recv.at[source],
            device_id=device,
            device_id_type=MESH,
        )

    def send_first(source, j):
        for u in range(1, side):
            map_copy(source, first_base + j * (side - 1) + u - 1, first_peer(u)).start()

    def send_second(source, j, u):
        for v in range(1, side):
            slot = second_base + (j * side + u) * (side - 1) + v - 1
            map_copy(source, slot, second_peer(v)).start()

    def back_copy(source, landed):
        return pltpu.make_async_remote_copy(
            src_ref=found.at[source],
            dst_ref=returned.at[landed],
            send_sem=back_send.at[source],
            recv_sem=back_recv.at[landed],
            device_id=place(source),
            device_id_type=MESH,
        )

    def raw_copy(image):
        return pltpu.make_async_copy(database_ref.at[image], raw.at[image], raw_sem.at[image])

    def slot_copy(parity):
        return pltpu.make_async_copy(
            slot_rows.at[parity], slot_table.at[parity], slot_sem.at[parity]
        )

    barrier = pltpu.get_barrier_semaphore()
    peers = [line_peer(j) for j in range(1, pb_count)]
    peers += [first_peer(u) for u in range(1, side)]
    peers += [second_peer(v) for v in range(1, side)]
    peers += [partner]
    for peer in peers:
        pl.semaphore_signal(barrier, inc=1, device_id=peer, device_id_type=MESH)

    query_copy = pltpu.make_async_copy(query_any.at[0], query_ref, query_sem)
    query_copy.start()

    @pl.loop(0, image_count)
    def _(image):
        raw_copy(image).start()

    my_info = shortlist_info(shortlist_ref[...], image_count, count)
    info[...] = my_info
    entries = my_info.shape[1]
    maps[me, cells : cells + TAIL, 0:entries] = my_info.astype(jnp.float32).astype(jnp.bfloat16)
    if maps.shape[2] > entries:
        maps[me, cells : cells + TAIL, entries:] = jnp.zeros(
            (TAIL, maps.shape[2] - entries), jnp.bfloat16
        )
    query_copy.wait()
    maps[me, 0:cells, :] = unit_map(query_ref[...].astype(jnp.float32)).T.astype(jnp.bfloat16)
    rank = lax.broadcasted_iota(jnp.int32, (ROWS, entries), 0)
    rank_value = rank.astype(jnp.float32)
    me_value = jnp.full((ROWS, entries), me, jnp.int32).astype(jnp.float32)

    def normalize(image):
        raw_copy(image).wait()
        units[image] = unit_map(raw[image].astype(jnp.float32)).astype(jnp.bfloat16)

    early = image_count // EARLY
    pl.loop(0, early)(normalize)
    pl.semaphore_wait(barrier, len(peers))

    send_first(me, 0)
    for j in range(1, pb_count):
        map_copy(me, j - 1, line_peer(j)).start()
    map_copy(me, partner_base, partner).start()

    fill_filters(query_taps, db_taps, filter_query, filter_db)
    peaks[...] = jnp.zeros_like(peaks)
    pl.loop(early, image_count)(normalize)

    def decode(turn):
        last = 2 * combos - 1
        odd = lax.rem(turn, 2)
        mid = jnp.where(odd == 1, (turn + 1) // 2, turn // 2 - 1)
        index = jnp.where(turn < 2, 0, jnp.where(turn == 2, 1, mid))
        index = jnp.where(turn == last, combos - 1, index)
        half = jnp.where((turn == 1) | (turn == last), 1, jnp.where(turn < 4, 0, 1 - odd))
        code = 0
        for n in range(combos):
            code = jnp.where(index == n, order[n], code)
        j = code // chips
        u = lax.rem(code // side, side)
        v = lax.rem(code, side)
        owner = lax.rem(core + half, 2)
        offset = u * (1 + owner * (side - 1)) + v * (side - owner * (side - 1))
        other_chip = flip(chip, offset, chips)
        source = (other_chip * 2 + owner) * pb_count + flip(pb, j, pb_count)
        return half, code, j, u, v, source

    def load_slots(source, parity):
        tail = maps[source, cells : cells + TAIL, 0:entries].astype(jnp.float32)
        hit = (tail[0:1, :] == me_value) & (tail[2:3, :] == rank_value)
        slot = jnp.sum(jnp.where(hit, tail[1:2, :], 0.0), axis=1, keepdims=True)
        slot_rows[parity] = jnp.broadcast_to(slot, (ROWS, entries)).astype(jnp.int32)
        slot_copy(parity).start()

    def serve(turn, half, code, j, u, v, source):
        map_copy(source, 0, partner).wait_recv()

        @pl.when(half == 0)
        def _():
            map_copy(source, partner_base + code, partner).start()

            @pl.when((u == 0) & (v == 0))
            def _():
                send_first(source, j)

            @pl.when(v == 0)
            def _():
                send_second(source, j, u)

        @pl.when(turn == 1)
        def _():
            send_second(me, 0, 0)

        load_slots(source, lax.rem(turn, 2))

    load_slots(me, 0)

    def step(turn, source):
        parity = lax.rem(turn, 2)
        coming = decode(turn + 1)
        upcoming = coming[-1]

        @pl.when((turn >= 3) & (turn + 1 < 2 * combos))
        def _():
            serve(turn + 1, *coming)

        slot_copy(parity).wait()
        for k in range(width):
            slot = jnp.clip(slot_table[parity, k, 0], 0, image_count - 1)
            correlation = jnp.dot(
                maps[source, 0:cells, :], units[slot], preferred_element_type=jnp.float32
            )
            positive[k] = jnp.maximum(correlation, 0.0).astype(jnp.bfloat16)
        for k in range(width):
            rectified = positive[k]
            filtered = jnp.dot(
                filter_query[...], rectified, preferred_element_type=jnp.float32
            ) + jnp.dot(rectified, filter_db[...], preferred_element_type=jnp.float32)
            peaks[k : k + 1, :] = jnp.max(filtered, axis=0, keepdims=True)
        best = peaks[...]
        total = jnp.sum(best, axis=1, keepdims=True) * (score_scale / best.shape[1])
        found[source] = jnp.broadcast_to(total, (ROWS, LANES))

        @pl.when(source != me)
        def _():
            back_copy(source, me).start()

        @pl.when(turn < 3)
        def _():
            serve(turn + 1, *coming)

        return upcoming

    lax.fori_loop(0, 2 * combos, step, me)

    returned[me] = found[me]

    @pl.loop(1, count)
    def _(step):
        other = lax.rem(me + step, count)
        back_copy(other, other).wait_recv()

    my_shard = info[0:1, :]
    my_bucket = info[2:3, :]
    scores = jnp.zeros((ROWS, LANES), jnp.float32)
    for s in range(count):
        scores = scores + jnp.where((my_shard == s) & (my_bucket == rank), returned[s], 0.0)
    final = jnp.sum(scores, axis=0, keepdims=True)
    out_ref[...] = final
    sorted_ref[...] = descending(final)

    @pl.loop(1, count)
    def _(step):
        back_copy(lax.rem(me + step, count), me).wait_send()

    @pl.loop(0, sends)
    def _(slot):
        map_copy(me, slot, partner).wait_send()


def body(db_count, pb_count, query_maps, database, shortlist, kernel_query, kernel_db):
    count = db_count * pb_count
    chips = db_count // 2
    side = math.isqrt(chips)
    sends = pb_count - 1 + pb_count * (side - 1) * (1 + side) + pb_count * chips
    image_count, channels, cells = database.shape
    entries = shortlist.shape[1]
    width = 2 * entries // count
    vmem = pl.BlockSpec(memory_space=pltpu.VMEM)
    whole = pl.BlockSpec(memory_space=pl.ANY)
    row = jax.ShapeDtypeStruct((1, entries), jnp.float32)
    scores, ordered = pl.pallas_call(
        functools.partial(kernel, db_count, pb_count, width),
        out_shape=(row, row),
        in_specs=[whole, vmem, whole, vmem, vmem],
        out_specs=(vmem, vmem),
        scratch_shapes=[
            pltpu.VMEM((cells, cells), jnp.bfloat16),
            pltpu.VMEM((cells, cells), jnp.bfloat16),
            pltpu.VMEM((image_count, channels, cells), jnp.bfloat16),
            pltpu.VMEM((width, cells, cells), jnp.bfloat16),
            pltpu.VMEM((count, cells + TAIL, channels), jnp.bfloat16),
            pltpu.VMEM((TAIL, entries), jnp.int32),
            pltpu.VMEM((image_count, channels, cells), jnp.bfloat16),
            pltpu.VMEM((2, ROWS, entries), jnp.int32),
            pltpu.SMEM((2, ROWS, entries), jnp.int32),
            pltpu.VMEM((ROWS, cells), jnp.float32),
            pltpu.VMEM((count, ROWS, LANES), jnp.float32),
            pltpu.VMEM((count, ROWS, LANES), jnp.float32),
            pltpu.VMEM((channels, cells), jnp.bfloat16),
            pltpu.SemaphoreType.DMA((sends,)),
            pltpu.SemaphoreType.DMA((count,)),
            pltpu.SemaphoreType.DMA((count,)),
            pltpu.SemaphoreType.DMA((count,)),
            pltpu.SemaphoreType.DMA((2,)),
            pltpu.SemaphoreType.DMA((image_count,)),
            pltpu.SemaphoreType.DMA,
        ],
        compiler_params=pltpu.CompilerParams(
            collective_id=0, has_side_effects=True, vmem_limit_bytes=56 * 1024 * 1024
        ),
    )(query_maps, shortlist, database, kernel_query, kernel_db)
    return (scores, ordered[:, :TOPK])


def solution(mesh):
    in_specs = (
        P(("db", "pb"), None, None),
        P(("db", "pb"), None, None),
        P(("db", "pb"), None),
        P(),
        P(),
    )
    out_specs = (P(("db", "pb"), None), P(("db", "pb"), None))
    step = functools.partial(body, mesh.shape["db"], mesh.shape["pb"])
    return jax.shard_map(step, mesh=mesh, in_specs=in_specs, out_specs=out_specs, check_vma=False)
```

time: 66.1 us -> 60.6 us (0.917)
  Pallas kernels: 63 us -> 57.4 us
    pallas_call x1, Pallas kernels: 63 us -> 57.4 us  [body(): pl.pallas_call(functools.partial(kernel, db_count, pb_count, width), out_...]
where the time goes in v1:
time: 60.6 us; the launch traced here: 60.3 us
  Pallas kernels  57.4 us (95%)
  local copies, waits for them, and re-layouts  2.25 us (4%)
  between operations  0.64 us (1%)
    pallas_call x1, Pallas kernels, body(): pl.pallas_call(functools.partial(kernel, db_count, pb_count, width), out_...  57.4 us
    unnamed x2, local copies, waits for them, and re-layouts  2.25 us

profile of v1, /device:TPU:0, one launch (start us, length us, event | category | flops | bytes accessed | tf_op | source)
XLA Modules:
  0.0 60.3 jit_solution(6887105302626690869)
XLA Ops:
  0.6 57.4 %shard_map.68 = (f32[1,128]{1,0:T(1,128)}, f32[1,128]{1,0:T(1,128)}) custom-call(bf16[1,256,256]{2,1,0:T(8,128)(2,1)} %query_any.1, s32[1,128]{1,0:T(1,128)} %shortlist_ref.1, bf16[32,256,256]{2,1,0:T(8,128)(2,1)} %database_ref.1, bf16[3,3]{1,0:T(4,128)(2,1)} %query_taps.1, bf16[3,3]{1,0:T(4,128)(2,1)} %db_taps.1), custom_call_target="tpu_custom_call" | custom-call | tf_op jit(solution)/shard_map/pallas_call | solution.py:369
  58.0 1.1 %copy.9 = f32[1,128]{1,0:T(1,128)} copy(f32[1,128]{1,0:T(1,128)} %get-tuple-element.8) | data formatting | bytes 1024
  59.1 1.1 %copy.10 = f32[1,100]{1,0:T(1,128)} copy(f32[1,100]{1,0:T(1,128)} %bitcast.1) | data formatting | bytes 800

commit v2 on v1

--- a/solution.py
+++ b/solution.py
@@ -85,14 +85,15 @@
 
 
 def combo_order(side, line):
-    order = []
-    for wave in range(line + 2):
-        for v in range(side):
-            for u in range(side):
-                j = wave - min(u, 1) - min(v, 1)
-                if 0 <= j < line:
-                    order.append((j * side + u) * side + v)
-    return order
+    ranked = []
+    for j in range(line):
+        arrival = 0 if j == 0 else (26 if j == 1 else 40 + 10 * j)
+        for u in range(side):
+            for v in range(side):
+                late = 1000 if j == 0 and u > 0 and v > 0 else 0
+                key = arrival + 25 * min(u, 1) + 30 * min(v, 1) + late
+                ranked.append((key, (j * side + u) * side + v))
+    return [code for _, code in sorted(ranked)]
 
 
 def kernel(
@@ -288,20 +289,22 @@
         def _():
             send_second(me, 0, 0)
 
-        load_slots(source, lax.rem(turn, 2))
-
     load_slots(me, 0)
 
-    def step(turn, source):
+    def step(ahead, turn, source):
         parity = lax.rem(turn, 2)
         coming = decode(turn + 1)
         upcoming = coming[-1]
 
-        @pl.when((turn >= 3) & (turn + 1 < 2 * combos))
-        def _():
-            serve(turn + 1, *coming)
+        if ahead:
+
+            @pl.when(turn + 1 < 2 * combos)
+            def _():
+                serve(turn + 1, *coming)
 
         slot_copy(parity).wait()
+        if ahead:
+            load_slots(upcoming, 1 - parity)
         for k in range(width):
             slot = jnp.clip(slot_table[parity, k, 0], 0, image_count - 1)
             correlation = jnp.dot(
@@ -322,13 +325,14 @@
         def _():
             back_copy(source, me).start()
 
-        @pl.when(turn < 3)
-        def _():
+        if not ahead:
             serve(turn + 1, *coming)
-
+            load_slots(upcoming, 1 - parity)
         return upcoming
 
-    lax.fori_loop(0, 2 * combos, step, me)
+    source = lax.fori_loop(0, 3, functools.partial(step, False), me)
+    lax.fori_loop(3, 2 * combos, functools.partial(step, True), source)
+    slot_copy(0).wait()
 
     returned[me] = found[me]
 

time: 60.6 us -> 57.3 us (0.946)
  Pallas kernels: 57.4 us -> 54.2 us
    pallas_call x1, Pallas kernels: 57.4 us -> 54.2 us  [body(): pl.pallas_call(functools.partial(kernel, db_count, pb_count, width), out_...]
where the time goes in v2:
time: 57.3 us; the launch traced here: 57.1 us
  Pallas kernels  54.2 us (95%)
  local copies, waits for them, and re-layouts  2.25 us (4%)
  between operations  0.64 us (1%)
    pallas_call x1, Pallas kernels, body(): pl.pallas_call(functools.partial(kernel, db_count, pb_count, width), out_...  54.2 us
    unnamed x2, local copies, waits for them, and re-layouts  2.25 us

profile of v2, /device:TPU:0, one launch (start us, length us, event | category | flops | bytes accessed | tf_op | source)
XLA Modules:
  0.0 57.1 jit_solution(129066550182575325)
XLA Ops:
  0.6 54.2 %shard_map.68 = (f32[1,128]{1,0:T(1,128)}, f32[1,128]{1,0:T(1,128)}) custom-call(bf16[1,256,256]{2,1,0:T(8,128)(2,1)} %query_any.1, s32[1,128]{1,0:T(1,128)} %shortlist_ref.1, bf16[32,256,256]{2,1,0:T(8,128)(2,1)} %database_ref.1, bf16[3,3]{1,0:T(4,128)(2,1)} %query_taps.1, bf16[3,3]{1,0:T(4,128)(2,1)} %db_taps.1), custom_call_target="tpu_custom_call" | custom-call | tf_op jit(solution)/shard_map/pallas_call | solution.py:373
  54.9 1.1 %copy.9 = f32[1,128]{1,0:T(1,128)} copy(f32[1,128]{1,0:T(1,128)} %get-tuple-element.8) | data formatting | bytes 1024
  56.0 1.1 %copy.10 = f32[1,100]{1,0:T(1,128)} copy(f32[1,100]{1,0:T(1,128)} %bitcast.1) | data formatting | bytes 800

commit v3 on v2

--- a/solution.py
+++ b/solution.py
@@ -13,7 +13,7 @@
 LANES = 128
 ROWS = 8
 TAIL = 16
-EARLY = 2
+EARLY = 8
 MESH = pl.DeviceIdType.MESH
 
 epsilon = 1e-06

time: 57.3 us -> 57.5 us (level)
  no operation moved by 1% of the time
where the time goes in v3:
time: 57.5 us; the launch traced here: 57.2 us
  Pallas kernels  54.3 us (94%)
  local copies, waits for them, and re-layouts  2.25 us (4%)
  between operations  0.64 us (1%)
    pallas_call x1, Pallas kernels, body(): pl.pallas_call(functools.partial(kernel, db_count, pb_count, width), out_...  54.3 us
    unnamed x2, local copies, waits for them, and re-layouts  2.25 us

profile of v3, /device:TPU:0, one launch (start us, length us, event | category | flops | bytes accessed | tf_op | source)
XLA Modules:
  0.0 57.2 jit_solution(1155142049283542926)
XLA Ops:
  0.6 54.3 %shard_map.68 = (f32[1,128]{1,0:T(1,128)}, f32[1,128]{1,0:T(1,128)}) custom-call(bf16[1,256,256]{2,1,0:T(8,128)(2,1)} %query_any.1, s32[1,128]{1,0:T(1,128)} %shortlist_ref.1, bf16[32,256,256]{2,1,0:T(8,128)(2,1)} %database_ref.1, bf16[3,3]{1,0:T(4,128)(2,1)} %query_taps.1, bf16[3,3]{1,0:T(4,128)(2,1)} %db_taps.1), custom_call_target="tpu_custom_call" | custom-call | tf_op jit(solution)/shard_map/pallas_call | solution.py:373
  55.0 1.1 %copy.9 = f32[1,128]{1,0:T(1,128)} copy(f32[1,128]{1,0:T(1,128)} %get-tuple-element.8) | data formatting | bytes 1024
  56.1 1.1 %copy.10 = f32[1,100]{1,0:T(1,128)} copy(f32[1,100]{1,0:T(1,128)} %bitcast.1) | data formatting | bytes 800
